TPU v7x, 32 devices: a whole 2x2x4 slice. The times are simulated.
32 devices in a mesh: dp: 4 (over y, core), tensor: 8 (over z, x).
Axes of the slice: x: 2, y: 2, z: 4, core: 2. Of those that a mesh axis runs over, the one named last changes fastest.
Arguments:
- patches: bfloat16 [32, 256, 1152], P('dp'), may hold values from -6 to 6
- conditioning: bfloat16 [32, 1152], P('dp'), may hold values from -6 to 6
- keep_count: int32 [32], P('dp'), may hold values from 64 to 192, as said below
- keep_index: int32 [32, 192], P('dp'), may hold values from 0 to 255, as said below
- mod_weight: bfloat16 [1152, 6912], P(None, 'tensor'), may hold values from -0.1875 to 0.1875
- mod_bias: bfloat16 [6912], P('tensor'), may hold values from -3 to 3
- qkv_weight: bfloat16 [3, 1152, 1152], P(None, None, 'tensor'), may hold values from -0.1875 to 0.1875
- qv_bias: bfloat16 [2, 1152], P(None, 'tensor'), may hold values from -3 to 3
- out_weight: bfloat16 [1152, 1152], P('tensor'), may hold values from -1.25 to 1.25
- out_bias: bfloat16 [1152], replicated, may hold values from -2 to 2
- up_weight: bfloat16 [1152, 4608], P(None, 'tensor'), may hold values from -0.1875 to 0.1875
- up_bias: bfloat16 [4608], P('tensor'), may hold values from -3 to 3
- down_weight: bfloat16 [4608, 1152], P('tensor'), may hold values from -0.09375 to 0.09375
- down_bias: bfloat16 [1152], replicated, may hold values from -2 to 2
- out_cotangent: bfloat16 [32, 192, 1152], P('dp'), may hold values from -6 to 6
Outputs:
- block_out: bfloat16 [32, 192, 1152], P('dp')
- grad_patches: bfloat16 [32, 256, 1152], P('dp')
- grad_conditioning: bfloat16 [32, 1152], P('dp')
- mod_weight_grad: float32 [1152, 6912], P(None, 'tensor')
- mod_bias_grad: float32 [6912], P('tensor')
- qkv_weight_grad: float32 [3, 1152, 1152], P(None, None, 'tensor')
- qv_bias_grad: float32 [2, 1152], P(None, 'tensor')
- out_weight_grad: float32 [1152, 1152], P('tensor')
- out_bias_grad: float32 [1152], replicated
- up_weight_grad: float32 [1152, 4608], P(None, 'tensor')
- up_bias_grad: float32 [4608], P('tensor')
- down_weight_grad: float32 [4608, 1152], P('tensor')
- down_bias_grad: float32 [1152], replicated
Inputs may be any that keep to these rules, and one draw needn't show every extreme that they name: `keep_count`: some image keeps 192 tokens and some keeps 64. A row of keep_index lists 192 different patch positions; the first keep_count of them are the image's kept tokens, the others are not read.
All inputs are finite; a program needn't handle non-finite values.
Results may differ from a plain program's by a relative error of at most 0.014.
The roundings to bfloat16 on the way count: a program that leaves them out, or rounds other values in their place, can miss the bound.
Values may be sent and summed in bfloat16 or wider, within the bound.
A program may use at most 192 MiB of HBM per device.

v0:
```python
import jax
import jax.numpy as jnp
from jax import lax
from jax.sharding import PartitionSpec as P

HD = 72


def layer_norm(inputs):
    centred = inputs - jnp.mean(inputs, axis=-1, keepdims=True)
    return centred * lax.rsqrt(jnp.mean(centred * centred, axis=-1, keepdims=True) + 1e-06)


def on_device(
    patches,
    conditioning,
    keep_count,
    keep_index,
    mod_weight,
    mod_bias,
    qkv_weight,
    qv_bias,
    out_weight,
    out_bias,
    up_weight,
    up_bias,
    down_weight,
    down_bias,
    out_cotangent,
):
    images, kept_rows = keep_index.shape
    model_width = patches.shape[2]
    local_width = qkv_weight.shape[2]
    local_heads = local_width // HD
    count_rows = images * kept_rows
    share_rows = kept_rows // lax.axis_size("tensor")
    share_start = lax.axis_index("tensor") * share_rows
    score_scale = HD ** (-0.5)
    live_rows = (jnp.arange(kept_rows, dtype=jnp.int32)[None, :] < keep_count[:, None]).astype(
        jnp.float32
    )[:, :, None]
    tokens = (
        jnp.take_along_axis(patches, keep_index[:, :, None], axis=1).astype(jnp.float32) * live_rows
    )
    cond_float = conditioning.astype(jnp.float32)
    silu_low = jax.nn.silu(cond_float).astype(jnp.bfloat16)
    mod_local = (
        jnp.dot(silu_low, mod_weight, preferred_element_type=jnp.float32)
        + mod_bias.astype(jnp.float32)
    ).astype(jnp.bfloat16)
    mod_full = lax.all_gather(mod_local, "tensor", axis=1, tiled=True).astype(jnp.float32)
    blocks = [
        mod_full[:, None, member * model_width : (member + 1) * model_width] for member in range(6)
    ]
    shift_one, scale_one, gate_one, shift_two, scale_two, gate_two = blocks
    norm_one = layer_norm(tokens)
    normed_one = (
        (norm_one * (1.0 + scale_one) + shift_one)
        .astype(jnp.bfloat16)
        .reshape(count_rows, model_width)
    )
    projected = jnp.einsum(
        "rd,tdh->trh", normed_one, qkv_weight, preferred_element_type=jnp.float32
    )
    bias_rows = jnp.stack([qv_bias[0], jnp.zeros_like(qv_bias[0]), qv_bias[1]]).astype(jnp.float32)[
        :, None, :
    ]
    qkv_rows = (projected + bias_rows).astype(jnp.bfloat16)
    queries, key_rows, value_rows = [
        qkv_rows[member].reshape(images, kept_rows, local_heads, HD) for member in range(3)
    ]
    key_live = live_rows[:, :, 0][:, None, None, :] > 0
    scores = (
        jnp.einsum("bqhd,bkhd->bhqk", queries, key_rows, preferred_element_type=jnp.float32)
        * score_scale
    )
    scores = jnp.where(key_live, scores, -1e30)
    row_top = jnp.max(scores, axis=-1, keepdims=True)
    exp_scores = jnp.exp(scores - row_top)
    row_total = jnp.sum(exp_scores, axis=-1, keepdims=True)
    log_total = row_top + jnp.log(row_total)
    weights_low = (exp_scores / row_total).astype(jnp.bfloat16)
    attended = jnp.einsum(
        "bhqk,bkhd->bqhd", weights_low, value_rows, preferred_element_type=jnp.float32
    )
    attended = attended.astype(jnp.bfloat16).reshape(count_rows, local_width)
    branch_part = jnp.dot(attended, out_weight, preferred_element_type=jnp.float32).reshape(
        images, kept_rows, model_width
    )
    out_bias_float = out_bias.astype(jnp.float32)
    branch = lax.psum(branch_part, "tensor") + out_bias_float
    middle = tokens + gate_one * branch
    norm_two = layer_norm(middle)
    normed_two = (norm_two * (1.0 + scale_two) + shift_two).astype(jnp.bfloat16)
    branch_share = lax.dynamic_slice_in_dim(branch, share_start, share_rows, 1)
    normed_rows = normed_two.reshape(count_rows, model_width)
    pre_act = jnp.dot(normed_rows, up_weight, preferred_element_type=jnp.float32) + up_bias.astype(
        jnp.float32
    )
    hidden = jax.nn.gelu(pre_act, approximate=True).astype(jnp.bfloat16)
    mlp_part = jnp.dot(hidden, down_weight, preferred_element_type=jnp.float32).reshape(
        images, kept_rows, model_width
    )
    down_bias_float = down_bias.astype(jnp.float32)
    mlp_out = (
        lax.psum(mlp_part.astype(jnp.bfloat16), "tensor").astype(jnp.float32) + down_bias_float
    )
    block_out = ((middle + gate_two * mlp_out) * live_rows).astype(jnp.bfloat16)
    mlp_share = lax.dynamic_slice_in_dim(mlp_out, share_start, share_rows, 1)
    grad_out = out_cotangent.astype(jnp.float32) * live_rows
    grad_share = lax.dynamic_slice_in_dim(grad_out, share_start, share_rows, 1)
    grad_gate_two = jnp.sum(grad_share * mlp_share, axis=1)
    grad_mlp = (gate_two * grad_out).astype(jnp.bfloat16).reshape(count_rows, model_width)
    down_bias_grad = jnp.sum(grad_mlp.astype(jnp.float32), axis=0)
    down_weight_grad = jnp.einsum("rf,rd->fd", hidden, grad_mlp, preferred_element_type=jnp.float32)
    grad_hidden = jnp.einsum("rd,fd->rf", grad_mlp, down_weight, preferred_element_type=jnp.float32)
    gelu_pull = jax.vjp(lambda inputs: jax.nn.gelu(inputs, approximate=True), pre_act)[1]
    grad_pre = gelu_pull(grad_hidden)[0].astype(jnp.bfloat16)
    up_bias_grad = jnp.sum(grad_pre.astype(jnp.float32), axis=0)
    up_weight_grad = jnp.einsum(
        "rd,rf->df", normed_rows, grad_pre, preferred_element_type=jnp.float32
    )
    grad_normed_two = jnp.einsum(
        "rf,df->rd", grad_pre, up_weight, preferred_element_type=jnp.float32
    ).reshape(images, kept_rows, model_width)
    grad_shift_two = jnp.sum(grad_normed_two, axis=1)
    grad_scale_two = jnp.sum(grad_normed_two * norm_two, axis=1)
    second_pull = jax.vjp(layer_norm, middle)[1]
    second_term = second_pull(grad_normed_two * (1.0 + scale_two))[0]
    grad_middle = grad_out + lax.psum(second_term, "tensor")
    grad_mid_share = lax.dynamic_slice_in_dim(grad_middle, share_start, share_rows, 1)
    grad_branch = (gate_one * grad_middle).astype(jnp.bfloat16)
    grad_gate_one = jnp.sum(grad_mid_share * branch_share, axis=1)
    grad_branch = grad_branch.reshape(count_rows, model_width)
    out_bias_grad = jnp.sum(grad_branch.astype(jnp.float32), axis=0)
    out_weight_grad = jnp.einsum(
        "rh,rd->hd", attended, grad_branch, preferred_element_type=jnp.float32
    )
    grad_att = jnp.einsum("rd,hd->rh", grad_branch, out_weight, preferred_element_type=jnp.float32)
    grad_att = grad_att.astype(jnp.bfloat16).reshape(images, kept_rows, local_heads, HD)
    scores_again = (
        jnp.einsum("bqhd,bkhd->bhqk", queries, key_rows, preferred_element_type=jnp.float32)
        * score_scale
    )
    weights_again = jnp.where(key_live, jnp.exp(scores_again - log_total), 0.0)
    grad_weights = jnp.einsum(
        "bqhd,bkhd->bhqk", grad_att, value_rows, preferred_element_type=jnp.float32
    )
    row_inner = jnp.sum(weights_again * grad_weights, axis=-1, keepdims=True)
    grad_scores = (weights_again * (grad_weights - row_inner)).astype(jnp.bfloat16)
    grad_values = jnp.einsum(
        "bhqk,bqhd->bkhd",
        weights_again.astype(jnp.bfloat16),
        grad_att,
        preferred_element_type=jnp.float32,
    )
    grad_queries = (
        jnp.einsum("bhqk,bkhd->bqhd", grad_scores, key_rows, preferred_element_type=jnp.float32)
        * score_scale
    )
    grad_keys = (
        jnp.einsum("bhqk,bqhd->bkhd", grad_scores, queries, preferred_element_type=jnp.float32)
        * score_scale
    )
    grad_qkv = jnp.stack(
        [
            member.reshape(count_rows, local_width)
            for member in (grad_queries, grad_keys, grad_values)
        ]
    ).astype(jnp.bfloat16)
    qkv_weight_grad = jnp.einsum(
        "rd,trh->tdh", normed_one, grad_qkv, preferred_element_type=jnp.float32
    )
    qv_bias_grad = jnp.stack(
        [
            jnp.sum(grad_qkv[0].astype(jnp.float32), axis=0),
            jnp.sum(grad_qkv[2].astype(jnp.float32), axis=0),
        ]
    )
    grad_normed_one = jnp.einsum(
        "trh,tdh->rd", grad_qkv, qkv_weight, preferred_element_type=jnp.float32
    ).reshape(images, kept_rows, model_width)
    grad_shift_one = jnp.sum(grad_normed_one, axis=1)
    grad_scale_one = jnp.sum(grad_normed_one * norm_one, axis=1)
    first_pull = jax.vjp(layer_norm, tokens)[1]
    first_term = first_pull(grad_normed_one * (1.0 + scale_one))[0]
    grad_tokens = (grad_middle + lax.psum(first_term, "tensor")) * live_rows
    grad_token_low = grad_tokens.astype(jnp.bfloat16)
    empty_grads = jnp.zeros(patches.shape, jnp.bfloat16)
    grad_patches = jax.vmap(
        lambda row_block, index_row, grad_block: row_block.at[index_row].set(grad_block)
    )(empty_grads, keep_index, grad_token_low)
    grad_mod_part = jnp.concatenate(
        [
            grad_shift_one,
            grad_scale_one,
            grad_gate_one,
            grad_shift_two,
            grad_scale_two,
            grad_gate_two,
        ],
        axis=1,
    )
    grad_mod = lax.psum_scatter(grad_mod_part, "tensor", scatter_dimension=1, tiled=True)
    silu_float = silu_low.astype(jnp.float32)
    mod_weight_grad = jnp.einsum("bd,bm->dm", silu_float, grad_mod, precision=lax.Precision.HIGHEST)
    mod_bias_grad = jnp.sum(grad_mod, axis=0)
    silu_term = jnp.einsum(
        "bm,dm->bd", grad_mod, mod_weight.astype(jnp.float32), precision=lax.Precision.HIGHEST
    )
    grad_silu = lax.psum(silu_term, "tensor")
    silu_pull = jax.vjp(jax.nn.silu, cond_float)[1]
    grad_conditioning = silu_pull(grad_silu)[0].astype(jnp.bfloat16)
    summed = (
        lax.psum(mod_weight_grad.astype(jnp.bfloat16), "dp").astype(jnp.float32),
        lax.psum(mod_bias_grad.astype(jnp.bfloat16), "dp").astype(jnp.float32),
        lax.psum(qkv_weight_grad.astype(jnp.bfloat16), "dp").astype(jnp.float32),
        lax.psum(qv_bias_grad.astype(jnp.bfloat16), "dp").astype(jnp.float32),
        lax.psum(out_weight_grad.astype(jnp.bfloat16), "dp").astype(jnp.float32),
        lax.psum(out_bias_grad.astype(jnp.bfloat16), "dp").astype(jnp.float32),
        lax.psum(up_weight_grad.astype(jnp.bfloat16), "dp").astype(jnp.float32),
        lax.psum(up_bias_grad.astype(jnp.bfloat16), "dp").astype(jnp.float32),
        lax.psum(down_weight_grad.astype(jnp.bfloat16), "dp").astype(jnp.float32),
        lax.psum(down_bias_grad.astype(jnp.bfloat16), "dp").astype(jnp.float32),
    )
    return (block_out, grad_patches, grad_conditioning) + tuple(summed)


def solution(mesh):
    placed = (
        P("dp", None, None),
        P("dp", None),
        P("dp"),
        P("dp", None),
        P(None, "tensor"),
        P("tensor"),
        P(None, None, "tensor"),
        P(None, "tensor"),
        P("tensor", None),
        P(),
        P(None, "tensor"),
        P("tensor"),
        P("tensor", None),
        P(),
        P("dp", None, None),
    )
    return jax.shard_map(
        on_device,
        mesh=mesh,
        in_specs=placed,
        out_specs=(
            P("dp", None, None),
            P("dp", None, None),
            P("dp", None),
            P(None, "tensor"),
            P("tensor"),
            P(None, None, "tensor"),
            P(None, "tensor"),
            P("tensor", None),
            P(),
            P(None, "tensor"),
            P("tensor"),
            P("tensor", None),
            P(),
        ),
        check_vma=False,
    )
```

profile of v0, /device:TPU:0, one launch (start us, length us, event | category | flops | bytes accessed | tf_op | source)
XLA Modules:
  0.0 1267.2 jit_solution(10761815162576918113)
XLA Ops:
  9.1 32.2 %gather_fusion = bf16[1536,1152]{1,0:T(8,128)(2,1)} fusion(bf16[8,256,1152]{2,1,0:T(8,128)(2,1)} %param.15, s32[1536]{0:T(1024)S(1)} %reshape.255), kind=kCustom, calls=%fused_computation | custom fusion | bytes 7090176 | tf_op jit(solution)/shard_map/jit(take_along_axis)/gather | solution.py:43
  41.3 2.8 fusion.5
  44.2 3.3 multiply_reduce_fusion.5
  48.2 32.4 %all-gather = bf16[8,864,8]{1,2,0:T(8,128)(2,1)S(1)} all-gather(bf16[1,864,8]{1,2,0:T(8,128)(2,1)S(1)} %fusion.46), channel_id=1, replica_groups=mesh['dp'=4,'tensor'=8] {'tensor'}, dimensions={0}, use_global_device_ids=true | all-gather | bytes 124416 | tf_op jit(solution)/shard_map/all_gather | solution.py:51
  81.0 4.4 fusion.3
  85.4 1.9 fusion.90
  90.3 1.7 reshape_squeeze.10
  95.5 4.2 fusion.61
  100.4 3.4 fusion.80
  103.8 1.7 copy-done.8
  105.6 4.3 fusion.91
  109.8 222.4 %all-reduce.8.cloned.1.call-done = f32[8,192,1152]{2,1,0:T(8,128)} async-done(((f32[8,192,1152]{2,1,0:T(8,128)}), f32[8,192,1152]{2,1,0:T(8,128)}) %all-reduce.8.cloned.1.call-update) | async-done | bytes 7077904 | tf_op jit(solution)/shard_map/psum | solution.py:91
  332.2 6.9 fusion.85
  340.0 1.9 copy-done.1
  342.0 1.6 add_convert_fusion
  344.4 5.8 fusion.81
  350.2 4.8 convolution_convert_fusion
  355.7 5.1 fusion.92
  360.8 6.3 multiply_reduce_fusion.3
  367.2 5.4 multiply_reduce_fusion
  372.6 120.3 %all-reduce.10.cloned.1.call-done = bf16[8,192,1152]{2,1,0:T(8,128)(2,1)} async-done(((bf16[8,192,1152]{2,1,0:T(8,128)(2,1)}), bf16[8,192,1152]{2,1,0:T(8,128)(2,1)}) %all-reduce.10.cloned.1.call-update) | async-done | bytes 3538960 | tf_op jit(solution)/shard_map/psum | solution.py:106
  493.0 17.5 %broadcast_add_fusion = (f32[8,192,1152]{2,1,0:T(8,128)}, bf16[8,192,1152]{2,1,0:T(8,128)(2,1)}, f32[8,192,1152]{2,1,0:T(8,128)}, f32[8,192,1152]{2,1,0:T(8,128)}) fusion(f32[8,192]{1,0:T(8,128)S(1)} %negate_multiply_fusion.1, f32[8,192]{1,0:T(8,128)S(1)} %multiply_multiply_fusion.4, f32[8,192,1152]{2,1,0:T(8,128)} %copy-done.1, ...), kind=kLoop, calls=%fused_computation.41 | loop fusion | flops 26542080 | bytes 46115328 | tf_op jit(solution)/shard_map/transpose(jvp())/add_any | solution.py:10
  512.2 6.2 convolution_convert_fusion.2
  518.4 4.2 convolution_convert_fusion.3
  524.2 217.0 %all-reduce.12.cloned.1.call-done = f32[8,192,1152]{2,1,0:T(8,128)} async-done(((f32[8,192,1152]{2,1,0:T(8,128)}), f32[8,192,1152]{2,1,0:T(8,128)}) %all-reduce.12.cloned.1.call-update) | async-done | bytes 7077904 | tf_op jit(solution)/shard_map/psum | solution.py:130
  741.2 7.3 fusion.83
  748.5 1.7 copy-done.6
  750.2 2.1 convolution_convert_fusion.5
  753.9 3.6 fusion.88
  757.4 1.6 multiply_reduce_fusion.6
  771.3 8.2 multiply_reduce_fusion.2
  780.8 3.8 convolution_convert_fusion.4
  784.6 5.8 fusion.1
  791.1 9.1 multiply_reduce_fusion.1
  805.5 3.2 copy.78
  809.1 4.8 fusion.19
  813.9 73.5 %reduce-scatter.4.cloned.1.call-done = f32[864,8]{1,0:T(8,128)} async-done(((f32[6912,8]{1,0:T(8,128)}), f32[864,8]{1,0:T(8,128)}) %reduce-scatter.4.cloned.1.call-update) | async-done | bytes 27664
  887.4 4.0 convolution_convert_fusion.1
  892.8 11.2 all-reduce
  907.9 36.0 %psum.109 = f32[8,1152]{1,0:T(8,128)S(1)} all-reduce(f32[8,1152]{1,0:T(8,128)S(1)} %fusion.58), channel_id=1, replica_groups=mesh['dp'=4,'tensor'=8] {'tensor'}, use_global_device_ids=true, to_apply=%region_23.24 | all-reduce | flops 9216 | bytes 73728 | tf_op jit(solution)/shard_map/psum | solution.py:211
  944.6 61.4 %all-reduce.16.cloned.1.call-done = (bf16[1152,864]{0,1:T(8,128)(2,1)}, bf16[3,1152,144]{1,2,0:T(8,128)(2,1)}, bf16[144,1152]{1,0:T(8,128)(2,1)}, bf16[1152,576]{0,1:T(8,128)(2,1)}, bf16[576,1152]{1,0:T(8,128)(2,1)}) async-done(((bf16[1152,864]{0,1:T(8,128)(2,1)}, bf16[3,1152,144]{1,2,0:T(8,128)(2,1)}, bf16[144,1152]{1,0:T(8,128)(2,1)}, bf16[1152,576]{0,1:T(8,128)(2,1)}, bf16[576,1152]{1,0:T(8,128)(2,1)}), ...) | async-done | bytes 5971984 | tf_op jit(solution)/shard_map/psum | solution.py:215
  1006.0 1.9 convert_element_type.235
  1008.0 3.9 convert_element_type.225
  1013.2 1.7 convert_element_type.238
  1014.9 1.7 convert_element_type.241
  1016.6 224.6 %all-reduce.14.cloned.1.call-done = f32[8,192,1152]{2,1,0:T(8,128)} async-done(((f32[8,192,1152]{2,1,0:T(8,128)}), f32[8,192,1152]{2,1,0:T(8,128)}) %all-reduce.14.cloned.1.call-update) | async-done | bytes 7077904 | tf_op jit(solution)/shard_map/psum | solution.py:187
  1241.2 7.4 multiply_convert_fusion
  1248.7 11.3 scatter_custom_fusion
  (185 shorter events, 44.2 us)
Async XLA Ops:
  7.2 40.4 %copy-start = (bf16[1152,864]{0,1:T(8,128)(2,1)S(1)}, bf16[1152,864]{0,1:T(8,128)(2,1)}, u32[]{:S(2)}) copy-start(bf16[1152,864]{0,1:T(8,128)(2,1)} %param.19) | copy-start | bytes 5971972
  7.2 325.1 %all-reduce.8.cloned.1.call-start = ((), (), s32[]{:S(2)}) async-start(), calls=%async_computation.1 | async-start | bytes 14155776 | tf_op jit(solution)/shard_map/psum | solution.py:91
  8.9 85.2 %copy-start.28 = (pred[8,192]{1,0:T(8,128)(4,1)}, pred[8,192]{1,0:T(8,128)(4,1)S(1)}, u32[]{:S(2)}) copy-start(pred[8,192]{1,0:T(8,128)(4,1)S(1)} %get-tuple-element.56) | copy-start | bytes 4612
  9.0 71.9 %copy-start.27 = (pred[1536]{0:T(1024)(128)(4,1)}, pred[1536]{0:T(1024)(128)(4,1)S(1)}, u32[]{:S(2)}) copy-start(pred[1536]{0:T(1024)(128)(4,1)S(1)} %broadcast_in_dim.78) | copy-start | bytes 4612
  41.3 6.2 copy-start.34
  41.3 6.2 copy-start.35
  41.3 6.2 copy-start.24
  81.0 4.5 copy-start.20
  85.4 1.9 copy-start.11
  90.2 2.9 copy-start.12
  92.0 2.1 copy-start.14
  92.0 2.1 copy-start.16
  93.1 2.3 copy-start.4
  94.1 1.4 copy-start.22
  99.7 393.3 %all-reduce.10.cloned.1.call-start = ((), (), s32[]{:S(2)}) async-start(), calls=%async_computation.2 | async-start | bytes 7077888 | tf_op jit(solution)/shard_map/psum | solution.py:106
  100.4 5.2 copy-start.41
  103.8 1.7 copy-start.8
  339.1 2.8 copy-start.1
  342.0 1.6 copy-start.43
  342.0 2.4 copy-start.45
  343.6 6.6 copy-start.10
  344.4 5.8 copy-start.42
  350.2 4.8 copy-start.46
  355.1 386.1 %all-reduce.12.cloned.1.call-start = ((), (), s32[]{:S(2)}) async-start(), calls=%async_computation.3 | async-start | bytes 14155776 | tf_op jit(solution)/shard_map/psum | solution.py:130
  360.8 6.4 copy-start.3
  510.5 376.9 %reduce-scatter.4.cloned.1.call-start = ((), (), s32[]{:S(2)}) async-start(), calls=%async_computation.5 | async-start | bytes 3981312
  512.1 6.2 copy-start.9
  512.2 6.2 copy-start.47
  524.1 226.1 %copy-start.23 = (bf16[144,1152]{1,0:T(8,128)(2,1)S(1)}, bf16[144,1152]{1,0:T(8,128)(2,1)}, u32[]{:S(2)}) copy-start(bf16[144,1152]{1,0:T(8,128)(2,1)} %param.23) | copy-start | bytes 995332
  748.5 1.7 copy-start.6
  748.5 5.4 copy-start.29
  752.3 5.2 copy-start.17
  753.8 3.6 copy-start.5
  759.1 1.2 copy-start.15
  759.1 2.7 copy-start.13
  780.1 4.4 copy-start.26
  780.8 3.8 copy-start.2
  808.8 197.2 %all-reduce.16.cloned.1.call-start = ((), (), s32[]{:S(2)}) async-start(), calls=%async_computation.6 | async-start | bytes 11943936 | tf_op jit(solution)/shard_map/psum | solution.py:215
  891.4 349.8 %all-reduce.14.cloned.1.call-start = ((), (), s32[]{:S(2)}) async-start(), calls=%async_computation.4 | async-start | bytes 14155776 | tf_op jit(solution)/shard_map/psum | solution.py:187
  891.5 0.9 copy-start.44
  891.5 1.0 copy-start.38
  891.5 1.1 copy-start.7
  891.5 1.3 copy-start.30
  891.5 1.3 copy-start.31
  891.5 1.3 copy-start.37
  1006.0 5.8 copy-start.21
  1008.0 5.3 copy-start.19
  1011.8 3.1 copy-start.18
  (6 other events, 4.2 us)
Sparse Core Ops, SparseCore 0:
  99.8 232.3 all-reduce.7
  355.2 137.7 all-reduce.9
  510.6 230.5 all-reduce.11
  808.9 78.4 reduce-scatter.3
  891.5 114.4 all-reduce.15
  1009.7 231.5 all-reduce.13
where the time goes:
time: 1280 us; the launch traced here: 1270 us
  waiting for transfers between devices  920 us (72%)
  other arithmetic  105 us (8%)
  blocking collectives  79.6 us (6%)
  local copies, waits for them, and re-layouts  74.9 us (6%)
  matrix products  71.1 us (6%)
  between operations  15.2 us (1%)
    psum x1, waiting for transfers between devices, on_device(): grad_tokens = (grad_middle + lax.psum(first_term, 'tensor')) * live_rows  225 us
    psum x1, waiting for transfers between devices, on_device(): branch = lax.psum(branch_part, 'tensor') + out_bias_float  222 us
    psum x1, waiting for transfers between devices, on_device(): grad_middle = grad_out + lax.psum(second_term, 'tensor')  217 us
    psum x1, waiting for transfers between devices, on_device(): lax.psum(mlp_part.astype(jnp.bfloat16), 'tensor').astype(jnp.float32)  120 us
    unnamed x7, waiting for transfers between devices  74 us
    psum x1, waiting for transfers between devices, on_device(): lax.psum(mod_weight_grad.astype(jnp.bfloat16), 'dp').astype(jnp.float32)  61.4 us
    psum x1, blocking collectives, on_device(): grad_silu = lax.psum(silu_term, 'tensor')  36 us
    all_gather x1, blocking collectives, on_device(): lax.all_gather(mod_local, 'tensor', axis=1, tiled=True).astype(jnp.float32)  32.4 us
  transfers between devices with their start and end apart: 6, of which 6 were waited for; matrix products, arithmetic and copies ran while one was open for 5% of the time, Pallas kernels for 0%

commit v1 on v0

--- a/solution.py
+++ b/solution.py
@@ -4,6 +4,14 @@
 from jax.sharding import PartitionSpec as P
 
 HD = 72
+
+
+def update_notes(x_part, row_axis):
+    lower = x_part
+    n_axis = lax.axis_size(row_axis)
+    for q in [b for b in (1, 2, 4, 8, 16) if b < n_axis]:
+        lower = lower + lax.ppermute(lower, row_axis, tuple(((c, c ^ q) for c in range(n_axis))))
+    return lower
 
 
 def layer_norm(inputs):
@@ -208,7 +216,7 @@
     silu_term = jnp.einsum(
         "bm,dm->bd", grad_mod, mod_weight.astype(jnp.float32), precision=lax.Precision.HIGHEST
     )
-    grad_silu = lax.psum(silu_term, "tensor")
+    grad_silu = update_notes(silu_term, "tensor")
     silu_pull = jax.vjp(jax.nn.silu, cond_float)[1]
     grad_conditioning = silu_pull(grad_silu)[0].astype(jnp.bfloat16)
     summed = (

time: 1280 us -> 1280 us (level)
  blocking collectives: 79.6 us -> 44.2 us
  waiting for transfers between devices: 920 us -> 950 us
    psum x1 -> x0, blocking collectives: 36 us -> none  [on_device(): grad_silu = lax.psum(silu_term, 'tensor')]
    psum x1, waiting for transfers between devices: 61.4 us -> 87.2 us  [on_device(): lax.psum(mod_weight_grad.astype(jnp.bfloat16), 'dp').astype(jnp.float32)]
  transfers between devices with their start and end apart: 6 -> 9, of which waited for: 6 -> 8; matrix products, arithmetic and copies ran while one was open for 5% -> 5% of each run, Pallas kernels for 0% -> 0%
where the time goes in v1:
time: 1280 us; the launch traced here: 1270 us
  waiting for transfers between devices  950 us (74%)
  other arithmetic  105 us (8%)
  local copies, waits for them, and re-layouts  75.1 us (6%)
  matrix products  71.1 us (6%)
  blocking collectives  44.2 us (3%)
  between operations  15.2 us (1%)
    psum x1, waiting for transfers between devices, on_device(): grad_tokens = (grad_middle + lax.psum(first_term, 'tensor')) * live_rows  225 us
    psum x1, waiting for transfers between devices, on_device(): branch = lax.psum(branch_part, 'tensor') + out_bias_float  222 us
    psum x1, waiting for transfers between devices, on_device(): grad_middle = grad_out + lax.psum(second_term, 'tensor')  217 us
    psum x1, waiting for transfers between devices, on_device(): lax.psum(mlp_part.astype(jnp.bfloat16), 'tensor').astype(jnp.float32)  120 us
    psum x1, waiting for transfers between devices, on_device(): lax.psum(mod_weight_grad.astype(jnp.bfloat16), 'dp').astype(jnp.float32)  87.2 us
    unnamed x7, waiting for transfers between devices  74 us
    all_gather x1, blocking collectives, on_device(): lax.all_gather(mod_local, 'tensor', axis=1, tiled=True).astype(jnp.float32)  32.4 us
    gather x3, local copies, waits for them, and re-layouts, on_device(): jnp.take_along_axis(patches, keep_index[:, :, None], axis=1)  32.3 us
  transfers between devices with their start and end apart: 9, of which 8 were waited for; matrix products, arithmetic and copies ran while one was open for 5% of the time, Pallas kernels for 0%

profile of v1, /device:TPU:0, one launch (start us, length us, event | category | flops | bytes accessed | tf_op | source)
XLA Modules:
  0.0 1267.4 jit_solution(10082893632976355354)
XLA Ops:
  9.1 32.2 %gather_fusion = bf16[1536,1152]{1,0:T(8,128)(2,1)} fusion(bf16[8,256,1152]{2,1,0:T(8,128)(2,1)} %param.15, s32[1536]{0:T(1024)S(1)} %reshape.255), kind=kCustom, calls=%fused_computation | custom fusion | bytes 7090176 | tf_op jit(solution)/shard_map/jit(take_along_axis)/gather | solution.py:51
  41.3 2.8 fusion.5
  44.2 3.3 multiply_reduce_fusion.5
  48.2 32.4 %all-gather = bf16[8,864,8]{1,2,0:T(8,128)(2,1)S(1)} all-gather(bf16[1,864,8]{1,2,0:T(8,128)(2,1)S(1)} %fusion.46), channel_id=1, replica_groups=mesh['dp'=4,'tensor'=8] {'tensor'}, dimensions={0}, use_global_device_ids=true | all-gather | bytes 124416 | tf_op jit(solution)/shard_map/all_gather | solution.py:59
  81.0 4.4 fusion.3
  85.4 1.9 fusion.90
  90.3 1.7 reshape_squeeze.10
  95.5 4.2 fusion.61
  100.4 3.4 fusion.80
  103.8 1.7 copy-done.8
  105.6 4.3 fusion.91
  109.8 222.4 %all-reduce.8.cloned.1.call-done = f32[8,192,1152]{2,1,0:T(8,128)} async-done(((f32[8,192,1152]{2,1,0:T(8,128)}), f32[8,192,1152]{2,1,0:T(8,128)}) %all-reduce.8.cloned.1.call-update) | async-done | bytes 7077904 | tf_op jit(solution)/shard_map/psum | solution.py:99
  332.2 6.9 fusion.85
  340.0 1.9 copy-done.1
  344.4 5.8 fusion.81
  350.2 4.8 convolution_convert_fusion
  355.7 5.1 fusion.92
  360.8 6.3 multiply_reduce_fusion.3
  367.2 5.4 multiply_reduce_fusion
  372.6 120.3 %all-reduce.10.cloned.1.call-done = bf16[8,192,1152]{2,1,0:T(8,128)(2,1)} async-done(((bf16[8,192,1152]{2,1,0:T(8,128)(2,1)}), bf16[8,192,1152]{2,1,0:T(8,128)(2,1)}) %all-reduce.10.cloned.1.call-update) | async-done | bytes 3538960 | tf_op jit(solution)/shard_map/psum | solution.py:114
  493.0 17.5 %broadcast_add_fusion = (f32[8,192,1152]{2,1,0:T(8,128)}, bf16[8,192,1152]{2,1,0:T(8,128)(2,1)}, f32[8,192,1152]{2,1,0:T(8,128)}, f32[8,192,1152]{2,1,0:T(8,128)}) fusion(f32[8,192]{1,0:T(8,128)S(1)} %negate_multiply_fusion.1, f32[8,192]{1,0:T(8,128)S(1)} %multiply_multiply_fusion.4, f32[8,192,1152]{2,1,0:T(8,128)} %copy-done.1, ...), kind=kLoop, calls=%fused_computation.41 | loop fusion | flops 26542080 | bytes 46115328 | tf_op jit(solution)/shard_map/transpose(jvp())/add_any | solution.py:18
  512.2 6.2 convolution_convert_fusion.2
  518.4 4.2 convolution_convert_fusion.3
  524.2 217.0 %all-reduce.12.cloned.1.call-done = f32[8,192,1152]{2,1,0:T(8,128)} async-done(((f32[8,192,1152]{2,1,0:T(8,128)}), f32[8,192,1152]{2,1,0:T(8,128)}) %all-reduce.12.cloned.1.call-update) | async-done | bytes 7077904 | tf_op jit(solution)/shard_map/psum | solution.py:138
  741.2 7.3 fusion.83
  748.5 1.7 copy-done.6
  750.2 2.1 convolution_convert_fusion.5
  753.9 3.6 fusion.88
  771.3 8.2 multiply_reduce_fusion.2
  780.8 3.8 convolution_convert_fusion.4
  784.6 5.8 fusion.1
  791.1 9.1 multiply_reduce_fusion.1
  805.5 3.2 copy.78
  809.1 4.8 fusion.19
  813.9 73.5 %reduce-scatter.4.cloned.1.call-done = f32[864,8]{1,0:T(8,128)} async-done(((f32[6912,8]{1,0:T(8,128)}), f32[864,8]{1,0:T(8,128)}) %reduce-scatter.4.cloned.1.call-update) | async-done | bytes 27664
  887.4 4.0 convolution_convert_fusion.1
  895.2 2.3 collective-permute-done
  899.0 2.4 collective-permute-done.1
  901.5 1.8 collective-permute-start.2
  903.5 11.8 all-reduce
  918.9 87.2 %all-reduce.16.cloned.1.call-done = (bf16[1152,864]{0,1:T(8,128)(2,1)}, bf16[3,1152,144]{1,2,0:T(8,128)(2,1)}, bf16[144,1152]{1,0:T(8,128)(2,1)}, bf16[1152,576]{0,1:T(8,128)(2,1)}, bf16[576,1152]{1,0:T(8,128)(2,1)}) async-done(((bf16[1152,864]{0,1:T(8,128)(2,1)}, bf16[3,1152,144]{1,2,0:T(8,128)(2,1)}, bf16[144,1152]{1,0:T(8,128)(2,1)}, bf16[1152,576]{0,1:T(8,128)(2,1)}, bf16[576,1152]{1,0:T(8,128)(2,1)}), ...) | async-done | bytes 5971984 | tf_op jit(solution)/shard_map/psum | solution.py:223
  1006.2 1.9 convert_element_type.235
  1008.1 3.9 convert_element_type.225
  1013.4 1.7 convert_element_type.238
  1015.1 1.7 convert_element_type.241
  1016.8 224.6 %all-reduce.14.cloned.1.call-done = f32[8,192,1152]{2,1,0:T(8,128)} async-done(((f32[8,192,1152]{2,1,0:T(8,128)}), f32[8,192,1152]{2,1,0:T(8,128)}) %all-reduce.14.cloned.1.call-update) | async-done | bytes 7077904 | tf_op jit(solution)/shard_map/psum | solution.py:195
  1241.4 7.4 multiply_convert_fusion
  1248.8 11.3 scatter_custom_fusion
  (192 shorter events, 50.7 us)
Async XLA Ops:
  7.2 40.4 %copy-start = (bf16[1152,864]{0,1:T(8,128)(2,1)S(1)}, bf16[1152,864]{0,1:T(8,128)(2,1)}, u32[]{:S(2)}) copy-start(bf16[1152,864]{0,1:T(8,128)(2,1)} %param.19) | copy-start | bytes 5971972
  7.2 325.1 %all-reduce.8.cloned.1.call-start = ((), (), s32[]{:S(2)}) async-start(), calls=%async_computation.1 | async-start | bytes 14155776 | tf_op jit(solution)/shard_map/psum | solution.py:99
  8.9 85.2 %copy-start.28 = (pred[8,192]{1,0:T(8,128)(4,1)}, pred[8,192]{1,0:T(8,128)(4,1)S(1)}, u32[]{:S(2)}) copy-start(pred[8,192]{1,0:T(8,128)(4,1)S(1)} %get-tuple-element.56) | copy-start | bytes 4612
  9.0 71.9 %copy-start.27 = (pred[1536]{0:T(1024)(128)(4,1)}, pred[1536]{0:T(1024)(128)(4,1)S(1)}, u32[]{:S(2)}) copy-start(pred[1536]{0:T(1024)(128)(4,1)S(1)} %broadcast_in_dim.78) | copy-start | bytes 4612
  41.3 6.2 copy-start.34
  41.3 6.2 copy-start.35
  41.3 6.2 copy-start.24
  81.0 4.5 copy-start.20
  85.4 1.9 copy-start.11
  90.2 2.9 copy-start.12
  92.0 2.1 copy-start.14
  92.0 2.1 copy-start.16
  93.1 2.3 copy-start.4
  99.7 393.3 %all-reduce.10.cloned.1.call-start = ((), (), s32[]{:S(2)}) async-start(), calls=%async_computation.2 | async-start | bytes 7077888 | tf_op jit(solution)/shard_map/psum | solution.py:114
  100.4 5.2 copy-start.41
  103.8 1.7 copy-start.8
  339.1 2.8 copy-start.1
  342.0 1.6 copy-start.43
  342.0 2.4 copy-start.45
  343.6 6.6 copy-start.10
  344.4 5.8 copy-start.42
  350.2 4.8 copy-start.46
  355.1 386.1 %all-reduce.12.cloned.1.call-start = ((), (), s32[]{:S(2)}) async-start(), calls=%async_computation.3 | async-start | bytes 14155776 | tf_op jit(solution)/shard_map/psum | solution.py:138
  360.8 6.4 copy-start.3
  510.5 376.9 %reduce-scatter.4.cloned.1.call-start = ((), (), s32[]{:S(2)}) async-start(), calls=%async_computation.5 | async-start | bytes 3981312
  512.1 6.2 copy-start.9
  512.2 6.2 copy-start.47
  524.1 226.1 %copy-start.23 = (bf16[144,1152]{1,0:T(8,128)(2,1)S(1)}, bf16[144,1152]{1,0:T(8,128)(2,1)}, u32[]{:S(2)}) copy-start(bf16[144,1152]{1,0:T(8,128)(2,1)} %param.23) | copy-start | bytes 995332
  748.5 1.7 copy-start.6
  748.5 5.4 copy-start.29
  752.3 5.2 copy-start.17
  753.8 3.6 copy-start.5
  759.1 2.7 copy-start.13
  780.1 4.4 copy-start.26
  780.8 3.8 copy-start.2
  808.8 197.4 %all-reduce.16.cloned.1.call-start = ((), (), s32[]{:S(2)}) async-start(), calls=%async_computation.6 | async-start | bytes 11943936 | tf_op jit(solution)/shard_map/psum | solution.py:223
  891.4 350.0 %all-reduce.14.cloned.1.call-start = ((), (), s32[]{:S(2)}) async-start(), calls=%async_computation.4 | async-start | bytes 14155776 | tf_op jit(solution)/shard_map/psum | solution.py:195
  891.5 3.6 copy-start.44
  891.5 3.6 copy-start.38
  891.5 12.0 copy-start.30
  891.5 12.0 copy-start.31
  891.5 12.0 copy-start.37
  893.5 4.0 collective-permute-start
  897.5 4.0 collective-permute-start.1
  901.5 16.8 %collective-permute-start.2 = (f32[8,1152]{1,0:T(8,128)S(1)}, f32[8,1152]{1,0:T(8,128)S(1)}, u32[]{:S(2)}, u32[]{:S(2)}) collective-permute-start(f32[8,1152]{1,0:T(8,128)S(1)} %add.220), channel_id=1, source_target_pairs={{0,4},{1,5},{2,6},{3,7},{4,0},{5,1},{6,2},{7,3},{8,12},{9,13},{10,... | collective-permute-start | bytes 110600 | tf_op jit(solution)/shard_map/ppermute | solution.py:13
  1006.2 5.8 copy-start.21
  1008.1 5.3 copy-start.19
  1012.0 3.1 copy-start.18
  (9 other events, 7.9 us)
Sparse Core Ops, SparseCore 0:
  99.8 232.3 all-reduce.7
  355.2 137.7 all-reduce.9
  510.6 230.5 all-reduce.11
  808.9 78.4 reduce-scatter.3
  891.5 114.5 all-reduce.15
  1009.8 231.5 all-reduce.13
